TPU v7x, 256 devices: a whole 4x4x8 slice. The times are simulated.
256 devices in a mesh: expert: 16 (over y, x), tensor: 16 (over z, core).
Axes of the slice: x: 4, y: 4, z: 8, core: 2. Of those that a mesh axis runs over, the one named last changes fastest.
Arguments:
- queries: bfloat16 [4096, 8192], P('expert', 'tensor'), may hold values from -8 to 8
- keys_values: bfloat16 [16, 4, 1280, 256], P('expert'), may hold values from -6 to 6
- prefix_len: int32 [16], P('expert'), may hold values from 128 to 1024, as said below
- out_proj: bfloat16 [8192, 4096], P('tensor', 'expert'), may hold values from -0.0625 to 0.0625
- residual: bfloat16 [4096, 4096], P(('expert', 'tensor')), may hold values from -1.796875 to 1.796875
- norm_gain: float32 [4096], replicated, may hold values from 0.1 to 1.9
- expert_ids: int32 [4096, 8], P('expert'), may hold values from 0 to 63, all different within a row; in each aligned block of 16 rows (0 to 15, 16 to 31, ...) at most 3 rows name the same one
- route_weights: bfloat16 [4096, 8], P('expert'), may hold values from 0.19921875 to 1
- w_gate: bfloat16 [256, 4096, 384], P(('expert', 'tensor')), may hold values from -0.09375 to 0.09375
- w_up: bfloat16 [256, 4096, 384], P(('expert', 'tensor')), may hold values from -0.09375 to 0.09375
- w_down: bfloat16 [256, 384, 4096], P(('expert', 'tensor')), may hold values from -0.15625 to 0.15625
Outputs:
- layer_out: bfloat16 [4096, 4096], P(('expert', 'tensor'))
Inputs may be any that keep to these rules, and one draw needn't show every extreme that they name: `expert_ids`: in the rows of one device (aligned blocks of 16 rows) no expert is named by more than 3 rows, a bound that some block reaches; a row names 8 different experts. `prefix_len`: some sequence has all 1024 slots live.
All inputs are finite; a program needn't handle non-finite values.
Results may differ from a plain program's by a relative error of at most 0.035.
Values may be sent and summed in bfloat16 or wider, within the bound.
No kernel may reach another device: no remote copies, remote signals or barrier semaphores. Data moves between devices by JAX's collectives and lax.ppermute only.
A program may use at most 128 MiB of HBM per device.

v0:
```python
import math
import jax
import jax.numpy as jnp
from jax import lax
from jax.sharding import PartitionSpec as P

HEADS = 64
KVH = 4
HD = 128
TOPK = 8
HSPLIT = 4
TOK_DEV = 16
PREFIX = 1024


def norm_rows(hidden_state, norm_gain):
    values = hidden_state.astype(jnp.float32)
    factor = lax.rsqrt(jnp.mean(values * values, axis=-1, keepdims=True) + 1e-06)
    return (values * factor * norm_gain[None, :]).astype(jnp.bfloat16)


def route_tables(expert_ids, route_weights, experts, most_rows):
    total_rows = expert_ids.shape[0]
    named_mask = expert_ids[:, :, None] == jnp.arange(experts, dtype=jnp.int32)[None, None, :]
    hit_table = jnp.sum(named_mask.astype(jnp.int32), axis=1)
    weight_table = jnp.sum(
        jnp.where(named_mask, route_weights[:, :, None].astype(jnp.float32), 0.0), axis=1
    )
    grouped = hit_table.reshape(total_rows // TOK_DEV, TOK_DEV, experts)
    rank_table = (jnp.cumsum(grouped, axis=1) - grouped).reshape(total_rows, experts)
    share_index = (jnp.arange(total_rows, dtype=jnp.int32) // TOK_DEV)[:, None]
    position_table = share_index * most_rows + rank_table
    return (hit_table, weight_table, rank_table, position_table)


def pick_slot(table, expert_count, slot_count, slot_index):
    shaped = table.reshape(table.shape[0], expert_count, slot_count)
    return lax.dynamic_index_in_dim(shaped, slot_index, 2, keepdims=False)


def shards(
    queries,
    keys_values,
    prefix_len,
    out_proj,
    residual,
    norm_gain,
    expert_ids,
    route_weights,
    w_gate,
    w_up,
    w_down,
):
    tensor_count = lax.axis_size("tensor")
    expert_count = lax.axis_size("expert")
    tensor_index = lax.axis_index("tensor")
    step_rows = queries.shape[0]
    per_device = queries.shape[1] // HD
    group_size = HEADS // KVH
    kv_index = tensor_index * per_device // group_size
    cached = lax.dynamic_index_in_dim(keys_values[0], kv_index, 0, keepdims=False)
    key_rows = cached[:, :HD]
    value_rows = cached[:, HD:]
    context = cached.shape[0]
    query_rows = queries.reshape(step_rows, per_device, HD)
    scores = jnp.einsum(
        "nhd,cd->hnc", query_rows, key_rows, preferred_element_type=jnp.float32
    ) / math.sqrt(HD)
    columns = jnp.arange(context, dtype=jnp.int32)[None, :]
    positions = jnp.arange(step_rows, dtype=jnp.int32)[:, None]
    visible = ((columns < prefix_len[0]) | (columns >= PREFIX) & (columns - PREFIX <= positions))[
        None
    ]
    highest = jnp.max(jnp.where(visible, scores, -1e30), axis=-1, keepdims=True)
    weights = jnp.exp(jnp.where(visible, scores - highest, -1e30))
    summed = jnp.sum(weights, axis=-1)
    blended = jnp.einsum(
        "hnc,cd->nhd", weights.astype(jnp.bfloat16), value_rows, preferred_element_type=jnp.float32
    )
    attended = (
        (blended / jnp.transpose(summed)[:, :, None])
        .astype(jnp.bfloat16)
        .reshape(step_rows, per_device * HD)
    )
    head_part = jnp.dot(
        attended,
        lax.all_gather(out_proj, "expert", axis=1, tiled=True),
        preferred_element_type=jnp.float32,
    )
    slot_count = tensor_count // HSPLIT
    experts = expert_count * slot_count
    most_rows = min(TOK_DEV, max(2, TOK_DEV * TOPK // experts + 1))
    capacity = tensor_count * most_rows
    slot_index = tensor_index // HSPLIT
    start_row = tensor_index * TOK_DEV
    hit_table, weight_table, rank_table, position_table = route_tables(
        expert_ids, route_weights, experts, most_rows
    )
    hit_slot = pick_slot(hit_table, expert_count, slot_count, slot_index)
    weight_slot = pick_slot(weight_table, expert_count, slot_count, slot_index)
    position_slot = pick_slot(position_table, expert_count, slot_count, slot_index)
    slot_match = (hit_slot[:, :, None] == 1) & (
        position_slot[:, :, None] == jnp.arange(capacity, dtype=jnp.int32)[None, None, :]
    )
    head_sum = lax.psum(head_part.astype(jnp.bfloat16), "tensor").astype(jnp.float32)
    residual_full = lax.all_gather(residual, "tensor", axis=0, tiled=True)
    state_full = (residual_full.astype(jnp.float32) + head_sum).astype(jnp.bfloat16)
    hidden_state = lax.dynamic_slice_in_dim(state_full, start_row, TOK_DEV, 0)
    normed_full = norm_rows(state_full, norm_gain)
    source_rows = jnp.sum(
        jnp.where(slot_match, jnp.arange(step_rows, dtype=jnp.int32)[:, None, None], 0), axis=0
    )
    filled = jnp.any(slot_match, axis=0)
    outgoing = jnp.where(
        filled[:, :, None], jnp.take(normed_full, source_rows, axis=0), jnp.zeros((), jnp.bfloat16)
    )
    arrived_rows = lax.all_to_all(outgoing, "expert", split_axis=0, concat_axis=0, tiled=True)
    flat_rows = arrived_rows.reshape(-1, arrived_rows.shape[-1])
    gate_val = jnp.dot(flat_rows, w_gate[0], preferred_element_type=jnp.float32)
    up_val = jnp.dot(flat_rows, w_up[0], preferred_element_type=jnp.float32)
    inner = (jax.nn.silu(gate_val) * up_val).astype(jnp.bfloat16)
    result = jnp.dot(inner, w_down[0], preferred_element_type=jnp.float32).astype(jnp.bfloat16)
    computed = result.reshape(arrived_rows.shape)
    returned = lax.all_to_all(computed, "expert", split_axis=0, concat_axis=0, tiled=True)
    combine_weights = jnp.where(slot_match, weight_slot[:, :, None], 0.0).astype(jnp.bfloat16)
    expert_part = jnp.einsum(
        "njc,jcd->nd", combine_weights, returned, preferred_element_type=jnp.float32
    )
    expert_share = lax.psum_scatter(
        expert_part.astype(jnp.bfloat16), "tensor", scatter_dimension=0, tiled=True
    ).astype(jnp.float32)
    return (hidden_state.astype(jnp.float32) + expert_share).astype(jnp.bfloat16)


def solution(mesh):
    return jax.shard_map(
        shards,
        mesh=mesh,
        in_specs=(
            P("expert", "tensor"),
            P("expert", None, None, None),
            P("expert"),
            P("tensor", "expert"),
            P(("expert", "tensor"), None),
            P(),
            P("expert", None),
            P("expert", None),
            P(("expert", "tensor"), None, None),
            P(("expert", "tensor"), None, None),
            P(("expert", "tensor"), None, None),
        ),
        out_specs=P(("expert", "tensor"), None),
        check_vma=False,
    )
```

profile of v0, /device:TPU:2, one launch (start us, length us, event | category | flops | bytes accessed | tf_op | source)
XLA Modules:
  0.0 520.2 jit_solution(15658658182001831944)
XLA Ops:
  6.5 0.7 all-gather.5.cloned.1.call-update
  7.3 0.7 all-gather.3.cloned.1.call-update
  8.1 0.8 convert_reduce_fusion
  8.9 0.1 copy.36
  9.7 1.1 copy.38
  10.7 1.9 reduce_window_sum.14
  12.7 2.0 dynamic-slice_bitcast_fusion
  14.7 1.0 fusion.26
  15.7 5.1 fusion.62
  20.8 2.4 fusion.33
  23.2 51.8 %all-gather.5.cloned.1.call-done = bf16[512,4096]{1,0:T(8,128)(2,1)} async-done(((bf16[512,256]{1,0:T(8,128)(2,1)}), bf16[512,4096]{1,0:T(8,128)(2,1)}) %all-gather.5.cloned.1.call-update) | async-done | bytes 4194320 | tf_op jit(solution)/shard_map/all_gather | solution.py:87
  75.0 4.8 convolution_convert_fusion.1
  79.8 0.9 fusion.57
  80.8 0.4 select_reduce_fusion
  81.2 0.1 reshape.155
  81.2 0.4 fusion.37
  81.6 34.7 %all-gather.3.cloned.1.call-done = bf16[256,4096]{1,0:T(8,128)(2,1)} async-done(((bf16[16,4096]{1,0:T(8,128)(2,1)}), bf16[256,4096]{1,0:T(8,128)(2,1)}) %all-gather.3.cloned.1.call-update) | async-done | bytes 2097168 | tf_op jit(solution)/shard_map/all_gather | solution.py:106
  116.4 115.7 %all-reduce.2.cloned.1.call-done = bf16[256,4096]{1,0:T(8,128)(2,1)} async-done(((bf16[256,4096]{1,0:T(8,128)(2,1)}), bf16[256,4096]{1,0:T(8,128)(2,1)}) %all-reduce.2.cloned.1.call-update) | async-done | bytes 2097168 | tf_op jit(solution)/shard_map/psum | solution.py:105
  232.1 3.2 fusion.6
  235.3 1.3 copy-done.1
  236.6 2.0 fusion.8
  238.6 13.8 %gather_fusion = bf16[768,4096]{1,0:T(8,128)(2,1)} fusion(bf16[256,4096]{1,0:T(8,128)(2,1)} %fusion.8, s32[1024]{0:T(1024)S(1)} %pad_clamp_fusion), kind=kCustom, calls=%fused_computation | custom fusion | bytes 12585984 | tf_op jit(solution)/shard_map/jit(_take)/gather | solution.py:115
  252.4 3.9 select_select_fusion
  256.3 79.0 %all_to_all.10 = bf16[16,48,4096]{2,1,0:T(8,128)(2,1)S(1)} all-to-all(bf16[16,48,4096]{2,1,0:T(8,128)(2,1)S(1)} %select_select_fusion), channel_id=1, replica_groups=mesh['expert'=16,'tensor'=16] {'expert'}, dimensions={0} | all-to-all | bytes 12582912 | tf_op jit(solution)/shard_map/all_to_all | solution.py:117
  335.3 3.4 fusion.12
  338.7 3.5 fusion.22
  342.2 5.4 %convolution_convert_fusion = bf16[768,4096]{1,0:T(8,128)(2,1)} fusion(bf16[768,384]{1,0:T(8,128)(2,1)S(1)} %fusion.22, bf16[1,384,4096]{2,1,0:T(8,128)(2,1)S(1)} %copy-done), kind=kOutput, calls=%fused_computation.2 | convolution fusion | flops 2419064832 | bytes 10027008 | tf_op jit(solution)/shard_map/dot_general | solution.py:122
  347.6 6.0 %all-to-all-start.1 = ((bf16[16,48,4096]{2,1,0:T(8,128)(2,1)}), bf16[16,48,4096]{2,1,0:T(8,128)(2,1)}, u32[]{:S(2)}, u32[]{:S(2)}) async-start(bf16[16,48,4096]{2,1,0:T(8,128)(2,1)} %bitcast.108), calls=%async_computation.1 | async-start | bytes 12582912 | tf_op jit(solution)/shard_map/all_to_all | solution.py:124
  353.8 87.2 %all-to-all-done.1 = bf16[16,48,4096]{2,1,0:T(8,128)(2,1)} async-done(((bf16[16,48,4096]{2,1,0:T(8,128)(2,1)}), bf16[16,48,4096]{2,1,0:T(8,128)(2,1)}, u32[]{:S(2)}, u32[]{:S(2)}) %all-to-all-start.1) | async-done | bytes 6291488 | tf_op jit(solution)/shard_map/all_to_all | solution.py:124
  441.0 6.0 %fusion.3 = bf16[256,4096]{1,0:T(8,128)(2,1)} fusion(bf16[16,48,4096]{2,1,0:T(8,128)(2,1)} %all-to-all-done.1, bf16[256,16]{0,1:T(8,128)(2,1)S(1)} %bitcast.119, s32[256,16]{0,1:T(8,128)S(1)} %bitcast.113, pred[256,16]{0,1:T(8,128)(4,1)S(1)} %bitcast.118), kind=kOutput, calls=%fused_computation.11 | convolution fusion | flops 1612251136 | bytes 8417280 | tf_op jit(solution)/shard_map/njc,jcd->nd/dot_general | solution.py:126
  447.0 65.0 %reduce-scatter.2.cloned.1.call-done = bf16[16,4096]{1,0:T(8,128)(2,1)} async-done(((bf16[256,4096]{1,0:T(8,128)(2,1)}), bf16[16,4096]{1,0:T(8,128)(2,1)}) %reduce-scatter.2.cloned.1.call-update) | async-done | bytes 131088 | tf_op jit(solution)/shard_map/reduce_scatter | solution.py:129
  512.0 1.7 add_convert_fusion.1
  (36 shorter events, 0.4 us)
Async XLA Ops:
  6.5 335.7 %copy-start = (bf16[1,384,4096]{2,1,0:T(8,128)(2,1)S(1)}, bf16[1,384,4096]{2,1,0:T(8,128)(2,1)}, u32[]{:S(2)}) copy-start(bf16[1,384,4096]{2,1,0:T(8,128)(2,1)} %param.21) | copy-start | bytes 9437188
  6.5 68.5 %all-gather.5.cloned.1.call-start = ((), (), s32[]{:S(2)}) async-start(), calls=%async_computation.4 | async-start | bytes 4456448 | tf_op jit(solution)/shard_map/all_gather | solution.py:87
  7.3 109.1 %all-gather.3.cloned.1.call-start = ((), (), s32[]{:S(2)}) async-start(), calls=%async_computation.3 | async-start | bytes 2228224 | tf_op jit(solution)/shard_map/all_gather | solution.py:106
  8.0 224.1 %all-reduce.2.cloned.1.call-start = ((), (), s32[]{:S(2)}) async-start(), calls=%async_computation.5 | async-start | bytes 4194304 | tf_op jit(solution)/shard_map/psum | solution.py:105
  79.8 156.8 %copy-start.3 = (f32[4096]{0:T(1024)S(1)}, f32[4096]{0:T(1024)}, u32[]{:S(2)}) copy-start(f32[4096]{0:T(1024)} %param.16) | copy-start | bytes 49156
  235.2 1.4 copy-start.1
  256.3 79.0 %copy-start.5 = (bf16[1,4096,384]{2,1,0:T(8,128)(2,1)S(1)}, bf16[1,4096,384]{2,1,0:T(8,128)(2,1)}, u32[]{:S(2)}) copy-start(bf16[1,4096,384]{2,1,0:T(8,128)(2,1)} %param.19) | copy-start | bytes 9437188
  335.3 3.4 copy-start.6
  347.6 6.0 %copy-start.4 = (bf16[256,8]{0,1:T(8,128)(2,1)S(1)}, bf16[256,8]{0,1:T(8,128)(2,1)}, u32[]{:S(2)}) copy-start(bf16[256,8]{0,1:T(8,128)(2,1)} %param.18) | copy-start | bytes 12292
  347.6 6.0 %copy-start.2 = (s32[256,8]{0,1:T(8,128)S(1)}, s32[256,8]{0,1:T(8,128)}, u32[]{:S(2)}) copy-start(s32[256,8]{0,1:T(8,128)} %param.17) | copy-start | bytes 24580
  347.6 93.4 %all-to-all-start.1 = ((bf16[16,48,4096]{2,1,0:T(8,128)(2,1)}), bf16[16,48,4096]{2,1,0:T(8,128)(2,1)}, u32[]{:S(2)}, u32[]{:S(2)}) async-start(bf16[16,48,4096]{2,1,0:T(8,128)(2,1)} %bitcast.108), calls=%async_computation.1 | async-start | bytes 12582912 | tf_op jit(solution)/shard_map/all_to_all | solution.py:124
  353.6 158.4 %reduce-scatter.2.cloned.1.call-start = ((), (), s32[]{:S(2)}) async-start(), calls=%async_computation.6 | async-start | bytes 2228224 | tf_op jit(solution)/shard_map/reduce_scatter | solution.py:129
Sparse Core Ops, SparseCore 0:
  9.8 65.2 all-gather.4
  76.8 39.4 all-gather.2
  118.7 113.3 all-reduce.1
  447.2 64.7 reduce-scatter.1
where the time goes:
time: 521 us; the launch traced here: 520 us
  waiting for transfers between devices  356 us (68%)
  blocking collectives  79 us (15%)
  matrix products  30.6 us (6%)
  local copies, waits for them, and re-layouts  20.5 us (4%)
  other arithmetic  14.3 us (3%)
  between operations  14 us (3%)
  starting transfers between devices  6.07 us (1%)
    psum x1, waiting for transfers between devices, shards(): lax.psum(head_part.astype(jnp.bfloat16), 'tensor').astype(jnp.float32)  116 us
    all_to_all x1, waiting for transfers between devices, shards(): lax.all_to_all(computed, 'expert', split_axis=0, concat_axis=0, tiled=True)  87.2 us
    all_to_all x1, blocking collectives, shards(): lax.all_to_all(outgoing, 'expert', split_axis=0, concat_axis=0, tiled=True)  79 us
    reduce_scatter x1, waiting for transfers between devices, shards(): lax.psum_scatter(expert_part.astype(jnp.bfloat16), 'tensor', scatter_dime...  65 us
    all_gather x1, waiting for transfers between devices, shards(): lax.all_gather(out_proj, 'expert', axis=1, tiled=True)  51.8 us
    all_gather x1, waiting for transfers between devices, shards(): residual_full = lax.all_gather(residual, 'tensor', axis=0, tiled=True)  34.7 us
    gather x1, local copies, waits for them, and re-layouts, shards(): jnp.take(normed_full, source_rows, axis=0)  13.8 us
  transfers between devices with their start and end apart: 5, of which 5 were waited for; matrix products, arithmetic and copies ran while one was open for 4% of the time, Pallas kernels for 0%

commit v1 on v0

--- a/solution.py
+++ b/solution.py
@@ -103,7 +103,26 @@
         position_slot[:, :, None] == jnp.arange(capacity, dtype=jnp.int32)[None, None, :]
     )
     head_sum = lax.psum(head_part.astype(jnp.bfloat16), "tensor").astype(jnp.float32)
-    residual_full = lax.all_gather(residual, "tensor", axis=0, tiled=True)
+    devices, index, rows = (lax.axis_size("tensor"), lax.axis_index("tensor"), residual.shape[0])
+    upward = [(i, (i + 1) % devices) for i in range(devices)]
+    left = [(i, (i - 1) % devices) for i in range(devices)]
+    whole = jnp.zeros(
+        (*residual.shape[:0], devices * rows, *residual.shape[0 + 1 :]), residual.dtype
+    )
+    whole = lax.dynamic_update_slice_in_dim(whole, residual, index * rows, axis=0)
+    from_left = from_right = residual
+    half = devices // 2
+    for lap in range(1, half + 1):
+        from_left = lax.ppermute(from_left, "tensor", upward)
+        whole = lax.dynamic_update_slice_in_dim(
+            whole, from_left, (index - lap) % devices * rows, axis=0
+        )
+        if lap < devices - half:
+            from_right = lax.ppermute(from_right, "tensor", left)
+            whole = lax.dynamic_update_slice_in_dim(
+                whole, from_right, (index + lap) % devices * rows, axis=0
+            )
+    residual_full = whole
     state_full = (residual_full.astype(jnp.float32) + head_sum).astype(jnp.bfloat16)
     hidden_state = lax.dynamic_slice_in_dim(state_full, start_row, TOK_DEV, 0)
     normed_full = norm_rows(state_full, norm_gain)

time: 521 us -> 484 us (0.929)
  waiting for transfers between devices: 356 us -> 279 us
  starting transfers between devices: 6.07 us -> 29.2 us
  local copies, waits for them, and re-layouts: 20.5 us -> 37.3 us
    all_gather x1, waiting for transfers between devices: 51.8 us -> 10.8 us  [shards(): lax.all_gather(out_proj, 'expert', axis=1, tiled=True)]
    all_gather x1 -> x0, waiting for transfers between devices: 34.7 us -> none  [shards(): residual_full = lax.all_gather(residual, 'tensor', axis=0, tiled=True)]
    ppermute x0 -> x15, starting transfers between devices: none -> 23.2 us  [the longest x7 23.1 us: shards(): from_right = lax.ppermute(from_right, 'tensor', left)]
    dynamic_update_slice x0 -> x16, local copies, waits for them, and re-layouts: none -> 15.9 us  [the longest x8 7.96 us: shards(): lax.dynamic_update_slice_in_dim(whole, from_left, (index - lap) % devices...]
    ppermute x0 -> x15, waiting for transfers between devices: none -> 5.74 us  [the longest x8 5.72 us: shards(): from_left = lax.ppermute(from_left, 'tensor', upward)]
    psum x1, waiting for transfers between devices: 116 us -> 110 us  [shards(): lax.psum(head_part.astype(jnp.bfloat16), 'tensor').astype(jnp.float32)]
  transfers between devices with their start and end apart: 5 -> 19, of which waited for: 5 -> 9; matrix products, arithmetic and copies ran while one was open for 4% -> 8% of each run, Pallas kernels for 0% -> 0%
where the time goes in v1:
time: 484 us; the launch traced here: 483 us
  waiting for transfers between devices  279 us (58%)
  blocking collectives  79 us (16%)
  local copies, waits for them, and re-layouts  37.3 us (8%)
  matrix products  30.7 us (6%)
  starting transfers between devices  29.2 us (6%)
  between operations  14.3 us (3%)
  other arithmetic  13.4 us (3%)
    psum x1, waiting for transfers between devices, shards(): lax.psum(head_part.astype(jnp.bfloat16), 'tensor').astype(jnp.float32)  110 us
    all_to_all x1, waiting for transfers between devices, shards(): lax.all_to_all(computed, 'expert', split_axis=0, concat_axis=0, tiled=True)  87.2 us
    all_to_all x1, blocking collectives, shards(): lax.all_to_all(outgoing, 'expert', split_axis=0, concat_axis=0, tiled=True)  79 us
    reduce_scatter x1, waiting for transfers between devices, shards(): lax.psum_scatter(expert_part.astype(jnp.bfloat16), 'tensor', scatter_dime...  65 us
    ppermute x7, starting transfers between devices, shards(): from_right = lax.ppermute(from_right, 'tensor', left)  23.1 us
    gather x1, local copies, waits for them, and re-layouts, shards(): jnp.take(normed_full, source_rows, axis=0)  13.8 us
    all_gather x1, waiting for transfers between devices, shards(): lax.all_gather(out_proj, 'expert', axis=1, tiled=True)  10.8 us
  transfers between devices with their start and end apart: 19, of which 9 were waited for; matrix products, arithmetic and copies ran while one was open for 8% of the time, Pallas kernels for 0%

profile of v1, /device:TPU:2, one launch (start us, length us, event | category | flops | bytes accessed | tf_op | source)
XLA Modules:
  0.0 482.9 jit_solution(11917246560910012783)
XLA Ops:
  6.5 5.3 %collective-permute-start.1 = (bf16[16,4096]{1,0:T(8,128)(2,1)}, bf16[16,4096]{1,0:T(8,128)(2,1)}, u32[]{:S(2)}, u32[]{:S(2)}) collective-permute-start(bf16[16,4096]{1,0:T(8,128)(2,1)} %param.15), channel_id=1, source_target_pairs={{0,15},{1,0},{2,1},{3,2},{4,3},{5,4},{6,5},{7,6},{8,7},{9,8},{10,9... | collective-permute-start | bytes 393224 | tf_op jit(solution)/shard_map/ppermute | solution.py:121
  16.7 2.0 dynamic-slice_bitcast_fusion
  19.7 5.1 %fusion.62 = (f32[4,256]{1,0:T(4,128)S(1)}, bf16[4,256,1280]{1,2,0:T(8,128)(2,1)}) fusion(pred[256,1280]{0,1:T(8,128)(4,1)S(1)} %fusion.26, bf16[1280,256]{1,0:T(8,128)(2,1)} %dynamic-slice_bitcast_fusion, bf16[256,512]{1,0:T(8,128)(2,1)} %param.11), kind=kOutput, calls=%fused_computation.100 | convolution fusion | flops 680264960 | bytes 4460544 | tf_op jit(solution)/shard_map/sub | solution.py:75
  24.8 2.5 fusion.33
  27.4 1.6 broadcast_in_dim.96
  30.0 2.9 collective-permute-start.3
  33.0 1.6 constant_dynamic-update-slice_fusion.14
  34.5 1.6 constant_dynamic-update-slice_fusion.13
  36.1 3.0 collective-permute-start.5
  41.7 3.0 collective-permute-start.7
  47.3 3.0 collective-permute-start.9
  52.9 3.0 collective-permute-start.11
  58.5 3.1 collective-permute-start.13
  62.3 1.6 constant_dynamic-update-slice_fusion.3
  64.2 10.8 %all-gather.2.cloned.1.call-done = bf16[512,4096]{1,0:T(8,128)(2,1)} async-done(((bf16[512,256]{1,0:T(8,128)(2,1)}), bf16[512,4096]{1,0:T(8,128)(2,1)}) %all-gather.2.cloned.1.call-update) | async-done | bytes 4194320 | tf_op jit(solution)/shard_map/all_gather | solution.py:87
  75.0 4.8 convolution_convert_fusion.1
  79.8 1.6 constant_dynamic-update-slice_fusion.2
  81.4 1.6 constant_dynamic-update-slice_fusion.1
  84.5 110.2 %all-reduce.2.cloned.1.call-done = bf16[256,4096]{1,0:T(8,128)(2,1)} async-done(((bf16[256,4096]{1,0:T(8,128)(2,1)}), bf16[256,4096]{1,0:T(8,128)(2,1)}) %all-reduce.2.cloned.1.call-update) | async-done | bytes 2097168 | tf_op jit(solution)/shard_map/psum | solution.py:105
  194.8 3.2 fusion.6
  199.3 2.0 fusion.8
  201.3 13.8 %gather_fusion = bf16[768,4096]{1,0:T(8,128)(2,1)} fusion(bf16[256,4096]{1,0:T(8,128)(2,1)} %fusion.8, s32[1024]{0:T(1024)S(1)} %pad_clamp_fusion), kind=kCustom, calls=%fused_computation | custom fusion | bytes 12585984 | tf_op jit(solution)/shard_map/jit(_take)/gather | solution.py:134
  215.1 3.9 select_select_fusion
  219.0 79.0 %all_to_all.10 = bf16[16,48,4096]{2,1,0:T(8,128)(2,1)S(1)} all-to-all(bf16[16,48,4096]{2,1,0:T(8,128)(2,1)S(1)} %select_select_fusion), channel_id=1, replica_groups=mesh['expert'=16,'tensor'=16] {'expert'}, dimensions={0} | all-to-all | bytes 12582912 | tf_op jit(solution)/shard_map/all_to_all | solution.py:136
  298.0 3.4 fusion.12
  301.4 3.5 fusion.22
  304.9 5.4 %convolution_convert_fusion = bf16[768,4096]{1,0:T(8,128)(2,1)} fusion(bf16[768,384]{1,0:T(8,128)(2,1)S(1)} %fusion.22, bf16[1,384,4096]{2,1,0:T(8,128)(2,1)S(1)} %copy-done), kind=kOutput, calls=%fused_computation.2 | convolution fusion | flops 2419064832 | bytes 10027008 | tf_op jit(solution)/shard_map/dot_general | solution.py:141
  310.3 6.0 %all-to-all-start.1 = ((bf16[16,48,4096]{2,1,0:T(8,128)(2,1)}), bf16[16,48,4096]{2,1,0:T(8,128)(2,1)}, u32[]{:S(2)}, u32[]{:S(2)}) async-start(bf16[16,48,4096]{2,1,0:T(8,128)(2,1)} %bitcast.108), calls=%async_computation.1 | async-start | bytes 12582912 | tf_op jit(solution)/shard_map/all_to_all | solution.py:143
  316.5 87.2 %all-to-all-done.1 = bf16[16,48,4096]{2,1,0:T(8,128)(2,1)} async-done(((bf16[16,48,4096]{2,1,0:T(8,128)(2,1)}), bf16[16,48,4096]{2,1,0:T(8,128)(2,1)}, u32[]{:S(2)}, u32[]{:S(2)}) %all-to-all-start.1) | async-done | bytes 6291488 | tf_op jit(solution)/shard_map/all_to_all | solution.py:143
  403.7 6.0 %fusion.3 = bf16[256,4096]{1,0:T(8,128)(2,1)} fusion(bf16[16,48,4096]{2,1,0:T(8,128)(2,1)} %all-to-all-done.1, bf16[256,16]{0,1:T(8,128)(2,1)S(1)} %bitcast.119, s32[256,16]{0,1:T(8,128)S(1)} %bitcast.113, pred[256,16]{0,1:T(8,128)(4,1)S(1)} %bitcast.118), kind=kOutput, calls=%fused_computation.11 | convolution fusion | flops 1612251136 | bytes 8417280 | tf_op jit(solution)/shard_map/njc,jcd->nd/dot_general | solution.py:145
  409.7 65.0 %reduce-scatter.2.cloned.1.call-done = bf16[16,4096]{1,0:T(8,128)(2,1)} async-done(((bf16[256,4096]{1,0:T(8,128)(2,1)}), bf16[16,4096]{1,0:T(8,128)(2,1)}) %reduce-scatter.2.cloned.1.call-update) | async-done | bytes 131088 | tf_op jit(solution)/shard_map/reduce_scatter | solution.py:148
  474.7 1.7 add_convert_fusion.1
  (82 shorter events, 20.7 us)
Async XLA Ops:
  6.5 298.3 %copy-start = (bf16[1,384,4096]{2,1,0:T(8,128)(2,1)S(1)}, bf16[1,384,4096]{2,1,0:T(8,128)(2,1)}, u32[]{:S(2)}) copy-start(bf16[1,384,4096]{2,1,0:T(8,128)(2,1)} %param.21) | copy-start | bytes 9437188
  6.5 68.5 %all-gather.2.cloned.1.call-start = ((), (), s32[]{:S(2)}) async-start(), calls=%async_computation.3 | async-start | bytes 4456448 | tf_op jit(solution)/shard_map/all_gather | solution.py:87
  6.5 23.4 %collective-permute-start = (bf16[16,4096]{1,0:T(8,128)(2,1)}, bf16[16,4096]{1,0:T(8,128)(2,1)}, u32[]{:S(2)}, u32[]{:S(2)}) collective-permute-start(bf16[16,4096]{1,0:T(8,128)(2,1)} %param.15), channel_id=1, source_target_pairs={{0,1},{1,2},{2,3},{3,4},{4,5},{5,6},{6,7},{7,8},{8,9},{9,10},{10,1... | collective-permute-start | bytes 393224 | tf_op jit(solution)/shard_map/ppermute | solution.py:116
  6.5 23.5 %collective-permute-start.1 = (bf16[16,4096]{1,0:T(8,128)(2,1)}, bf16[16,4096]{1,0:T(8,128)(2,1)}, u32[]{:S(2)}, u32[]{:S(2)}) collective-permute-start(bf16[16,4096]{1,0:T(8,128)(2,1)} %param.15), channel_id=1, source_target_pairs={{0,15},{1,0},{2,1},{3,2},{4,3},{5,4},{6,5},{7,6},{8,7},{9,8},{10,9... | collective-permute-start | bytes 393224 | tf_op jit(solution)/shard_map/ppermute | solution.py:121
  11.9 182.9 %all-reduce.2.cloned.1.call-start = ((), (), s32[]{:S(2)}) async-start(), calls=%async_computation.4 | async-start | bytes 4194304 | tf_op jit(solution)/shard_map/psum | solution.py:105
  24.8 4.1 copy-start.2
  30.0 6.1 %collective-permute-start.2 = (bf16[16,4096]{1,0:T(8,128)(2,1)}, bf16[16,4096]{1,0:T(8,128)(2,1)S(1)}, u32[]{:S(2)}, u32[]{:S(2)}) collective-permute-start(bf16[16,4096]{1,0:T(8,128)(2,1)} %collective-permute-done), channel_id=1, source_target_pairs={{0,1},{1,2},{2,3},{3,4},{4,5},{5,6},{6,7},{7,8},{8,9},{9,10},{10,1... | collective-permute-start | bytes 393224 | tf_op jit(solution)/shard_map/ppermute | solution.py:116
  30.0 6.1 %collective-permute-start.3 = (bf16[16,4096]{1,0:T(8,128)(2,1)}, bf16[16,4096]{1,0:T(8,128)(2,1)S(1)}, u32[]{:S(2)}, u32[]{:S(2)}) collective-permute-start(bf16[16,4096]{1,0:T(8,128)(2,1)} %collective-permute-done.1), channel_id=1, source_target_pairs={{0,15},{1,0},{2,1},{3,2},{4,3},{5,4},{6,5},{7,6},{8,7},{9,8},{10,9... | collective-permute-start | bytes 393224 | tf_op jit(solution)/shard_map/ppermute | solution.py:121
  36.1 5.6 %collective-permute-start.4 = (bf16[16,4096]{1,0:T(8,128)(2,1)S(1)}, bf16[16,4096]{1,0:T(8,128)(2,1)S(1)}, u32[]{:S(2)}, u32[]{:S(2)}) collective-permute-start(bf16[16,4096]{1,0:T(8,128)(2,1)S(1)} %collective-permute-done.2), channel_id=1, source_target_pairs={{0,1},{1,2},{2,3},{3,4},{4,5},{5,6},{6,7},{7,8},{8,9},{9,10},{10,1... | collective-permute-start | bytes 393224 | tf_op jit(solution)/shard_map/ppermute | solution.py:116
  36.1 5.6 %collective-permute-start.5 = (bf16[16,4096]{1,0:T(8,128)(2,1)S(1)}, bf16[16,4096]{1,0:T(8,128)(2,1)S(1)}, u32[]{:S(2)}, u32[]{:S(2)}) collective-permute-start(bf16[16,4096]{1,0:T(8,128)(2,1)S(1)} %collective-permute-done.3), channel_id=1, source_target_pairs={{0,15},{1,0},{2,1},{3,2},{4,3},{5,4},{6,5},{7,6},{8,7},{9,8},{10,9... | collective-permute-start | bytes 393224 | tf_op jit(solution)/shard_map/ppermute | solution.py:121
  41.7 5.6 %collective-permute-start.6 = (bf16[16,4096]{1,0:T(8,128)(2,1)S(1)}, bf16[16,4096]{1,0:T(8,128)(2,1)S(1)}, u32[]{:S(2)}, u32[]{:S(2)}) collective-permute-start(bf16[16,4096]{1,0:T(8,128)(2,1)S(1)} %collective-permute-done.4), channel_id=1, source_target_pairs={{0,1},{1,2},{2,3},{3,4},{4,5},{5,6},{6,7},{7,8},{8,9},{9,10},{10,1... | collective-permute-start | bytes 393224 | tf_op jit(solution)/shard_map/ppermute | solution.py:116
  41.7 5.6 %collective-permute-start.7 = (bf16[16,4096]{1,0:T(8,128)(2,1)S(1)}, bf16[16,4096]{1,0:T(8,128)(2,1)S(1)}, u32[]{:S(2)}, u32[]{:S(2)}) collective-permute-start(bf16[16,4096]{1,0:T(8,128)(2,1)S(1)} %collective-permute-done.5), channel_id=1, source_target_pairs={{0,15},{1,0},{2,1},{3,2},{4,3},{5,4},{6,5},{7,6},{8,7},{9,8},{10,9... | collective-permute-start | bytes 393224 | tf_op jit(solution)/shard_map/ppermute | solution.py:121
  47.3 5.6 %collective-permute-start.8 = (bf16[16,4096]{1,0:T(8,128)(2,1)S(1)}, bf16[16,4096]{1,0:T(8,128)(2,1)S(1)}, u32[]{:S(2)}, u32[]{:S(2)}) collective-permute-start(bf16[16,4096]{1,0:T(8,128)(2,1)S(1)} %collective-permute-done.6), channel_id=1, source_target_pairs={{0,1},{1,2},{2,3},{3,4},{4,5},{5,6},{6,7},{7,8},{8,9},{9,10},{10,1... | collective-permute-start | bytes 393224 | tf_op jit(solution)/shard_map/ppermute | solution.py:116
  47.3 5.6 %collective-permute-start.9 = (bf16[16,4096]{1,0:T(8,128)(2,1)S(1)}, bf16[16,4096]{1,0:T(8,128)(2,1)S(1)}, u32[]{:S(2)}, u32[]{:S(2)}) collective-permute-start(bf16[16,4096]{1,0:T(8,128)(2,1)S(1)} %collective-permute-done.7), channel_id=1, source_target_pairs={{0,15},{1,0},{2,1},{3,2},{4,3},{5,4},{6,5},{7,6},{8,7},{9,8},{10,9... | collective-permute-start | bytes 393224 | tf_op jit(solution)/shard_map/ppermute | solution.py:121
  52.9 5.6 %collective-permute-start.10 = (bf16[16,4096]{1,0:T(8,128)(2,1)S(1)}, bf16[16,4096]{1,0:T(8,128)(2,1)S(1)}, u32[]{:S(2)}, u32[]{:S(2)}) collective-permute-start(bf16[16,4096]{1,0:T(8,128)(2,1)S(1)} %collective-permute-done.8), channel_id=1, source_target_pairs={{0,1},{1,2},{2,3},{3,4},{4,5},{5,6},{6,7},{7,8},{8,9},{9,10},{10,1... | collective-permute-start | bytes 393224 | tf_op jit(solution)/shard_map/ppermute | solution.py:116
  52.9 5.6 %collective-permute-start.11 = (bf16[16,4096]{1,0:T(8,128)(2,1)S(1)}, bf16[16,4096]{1,0:T(8,128)(2,1)}, u32[]{:S(2)}, u32[]{:S(2)}) collective-permute-start(bf16[16,4096]{1,0:T(8,128)(2,1)S(1)} %collective-permute-done.9), channel_id=1, source_target_pairs={{0,15},{1,0},{2,1},{3,2},{4,3},{5,4},{6,5},{7,6},{8,7},{9,8},{10,9... | collective-permute-start | bytes 393224 | tf_op jit(solution)/shard_map/ppermute | solution.py:121
  58.5 5.7 %collective-permute-start.12 = (bf16[16,4096]{1,0:T(8,128)(2,1)S(1)}, bf16[16,4096]{1,0:T(8,128)(2,1)}, u32[]{:S(2)}, u32[]{:S(2)}) collective-permute-start(bf16[16,4096]{1,0:T(8,128)(2,1)S(1)} %collective-permute-done.10), channel_id=1, source_target_pairs={{0,1},{1,2},{2,3},{3,4},{4,5},{5,6},{6,7},{7,8},{8,9},{9,10},{10,1... | collective-permute-start | bytes 393224 | tf_op jit(solution)/shard_map/ppermute | solution.py:116
  58.5 22.9 %collective-permute-start.13 = (bf16[16,4096]{1,0:T(8,128)(2,1)}, bf16[16,4096]{1,0:T(8,128)(2,1)}, u32[]{:S(2)}, u32[]{:S(2)}) collective-permute-start(bf16[16,4096]{1,0:T(8,128)(2,1)} %collective-permute-done.11), channel_id=1, source_target_pairs={{0,15},{1,0},{2,1},{3,2},{4,3},{5,4},{6,5},{7,6},{8,7},{9,8},{10,9... | collective-permute-start | bytes 393224 | tf_op jit(solution)/shard_map/ppermute | solution.py:121
  64.2 18.7 %collective-permute-start.14 = (bf16[16,4096]{1,0:T(8,128)(2,1)}, bf16[16,4096]{1,0:T(8,128)(2,1)}, u32[]{:S(2)}, u32[]{:S(2)}) collective-permute-start(bf16[16,4096]{1,0:T(8,128)(2,1)} %collective-permute-done.12), channel_id=1, source_target_pairs={{0,1},{1,2},{2,3},{3,4},{4,5},{5,6},{6,7},{7,8},{8,9},{9,10},{10,1... | collective-permute-start | bytes 393224 | tf_op jit(solution)/shard_map/ppermute | solution.py:116
  84.5 114.7 %copy-start.4 = (f32[4096]{0:T(1024)S(1)}, f32[4096]{0:T(1024)}, u32[]{:S(2)}) copy-start(f32[4096]{0:T(1024)} %param.16) | copy-start | bytes 49156
  197.9 1.3 copy-start.1
  219.0 79.0 %copy-start.6 = (bf16[1,4096,384]{2,1,0:T(8,128)(2,1)S(1)}, bf16[1,4096,384]{2,1,0:T(8,128)(2,1)}, u32[]{:S(2)}) copy-start(bf16[1,4096,384]{2,1,0:T(8,128)(2,1)} %param.19) | copy-start | bytes 9437188
  298.0 3.4 copy-start.7
  310.3 6.0 %copy-start.5 = (bf16[256,8]{0,1:T(8,128)(2,1)S(1)}, bf16[256,8]{0,1:T(8,128)(2,1)}, u32[]{:S(2)}) copy-start(bf16[256,8]{0,1:T(8,128)(2,1)} %param.18) | copy-start | bytes 12292
  310.3 6.0 %copy-start.3 = (s32[256,8]{0,1:T(8,128)S(1)}, s32[256,8]{0,1:T(8,128)}, u32[]{:S(2)}) copy-start(s32[256,8]{0,1:T(8,128)} %param.17) | copy-start | bytes 24580
  310.3 93.4 %all-to-all-start.1 = ((bf16[16,48,4096]{2,1,0:T(8,128)(2,1)}), bf16[16,48,4096]{2,1,0:T(8,128)(2,1)}, u32[]{:S(2)}, u32[]{:S(2)}) async-start(bf16[16,48,4096]{2,1,0:T(8,128)(2,1)} %bitcast.108), calls=%async_computation.1 | async-start | bytes 12582912 | tf_op jit(solution)/shard_map/all_to_all | solution.py:143
  316.3 158.4 %reduce-scatter.2.cloned.1.call-start = ((), (), s32[]{:S(2)}) async-start(), calls=%async_computation.5 | async-start | bytes 2228224 | tf_op jit(solution)/shard_map/reduce_scatter | solution.py:148
Sparse Core Ops, SparseCore 0:
  12.0 62.9 all-gather.1
  80.0 114.7 all-reduce.1
  409.8 64.7 reduce-scatter.1
